TPU v7x, 32 devices: a whole 2x2x4 slice. The times are simulated.
32 devices in a mesh: occ: 8 (over z, x), aux: 4 (over y, core).
Axes of the slice: x: 2, y: 2, z: 4, core: 2. Of those that a mesh axis runs over, the one named last changes fastest.
Arguments:
- three_index: bfloat16 [8, 448, 1536], P('occ', None, 'aux'), may hold values from -0.75 to 0.75
- occ_energy: float32 [8], P('occ'), may hold values from -2 to -0.3
- vir_energy: float32 [448], replicated, may hold values from 0.3 to 3
Outputs:
- gamma: float32 [8, 448, 1536], P('occ', None, 'aux')
All inputs are finite; a program needn't handle non-finite values.
Results may differ from a plain program's by a relative error of at most 0.0019.
Values may be sent and summed in bfloat16 or wider, within the bound.
A program may use at most 64 MiB of HBM per device.

v0:
```python
import functools
import heapq

import jax
import jax.numpy as jnp
from jax import lax
from jax.experimental import pallas as pl
from jax.experimental.pallas import tpu as pltpu
from jax.sharding import PartitionSpec as P

MESH = pl.DeviceIdType.MESH
CORES = 2
GATHER_LIMIT = 24 * 1024 * 1024
PIECES = ((0.145, "yxz"), (0.43, "zyx"), (0.43, "zxy"))
RATE = {"x": 46.0, "y": 46.0, "z": 25.0, "c": 150.0}
HOP = {"x": 1700.0, "y": 1700.0, "z": 1700.0, "c": 900.0}


def from_behind(array, axis, by):
    size = lax.axis_size(axis)
    return lax.ppermute(array, axis, [(i, (i + by) % size) for i in range(size)])


def reach(size):
    return {1: size // 2, -1: (size - 1) // 2}


def piece_rows(rows):
    pieces, low = [], 0
    for at, (share, order) in enumerate(PIECES):
        count = int(rows * share) // 16 * 16
        if at == len(PIECES) - 1:
            count = rows - low
        pieces.append((low, count, order))
        low += count
    return pieces


def moves(rel, arrived, order, sizes, flip):
    out = []
    first = 0
    if arrived is not None:
        way = 1 if rel[arrived] > 0 else -1
        if abs(rel[arrived]) < reach(sizes[arrived])[way]:
            out.append((arrived, way))
        first = order.index(arrived) + 1
    for dim in order[first:]:
        for way in (1, -1):
            if reach(sizes[dim])[way] >= 1:
                out.append((dim, way))
    return out


def plan(rows, width, sizes):
    pieces = piece_rows(rows)
    free = {}
    heap, count = [], 0
    for at, (_, _, order) in enumerate(pieces):
        heap.append((0.0, count, at, (0, 0, 0), None, "own"))
        count += 1
    heapq.heapify(heap)
    events = []

    def queue(link, now, size):
        start = max(now, free.get(link, 0.0))
        free[link] = start + size / RATE[link[0]]
        return free[link] + HOP[link[0]]

    while heap:
        now, _, at, rel, arrived, kind = heapq.heappop(heap)
        low, number, order = pieces[at]
        size = number * width * 2
        if kind == "core":
            events.append((now, at, rel, "core", ()))
            continue
        named = dict(zip("xyz", rel))
        onward = moves(named, arrived, order, sizes, None)
        sends = []
        for dim, way in onward:
            when = queue((dim, way), now, size)
            after = dict(named)
            after[dim] += way
            heapq.heappush(heap, (when, count, at, (after["x"], after["y"], after["z"]), dim, "link"))
            count += 1
            sends.append((dim, way))
        when = queue(("c", 1), now, size)
        heapq.heappush(heap, (when, count, at, rel, None, "core"))
        count += 1
        events.append((now, at, rel, kind, tuple(sends)))
    return pieces, events


def gather_kernel(nz, nx, ny, b_ref, e_ref, col_ref, row_ref, out_ref, blocks, energies,
                  send_sem, recv_sem, esend_sem, erecv_sem, own_sem):
    rows, width = b_ref.shape
    occ, aux = lax.axis_index("occ"), lax.axis_index("aux")
    z, x = occ // nx, occ % nx
    y, core = aux // CORES, aux % CORES
    sizes = {"x": nx, "y": ny, "z": nz}
    turn = 1 - 2 * core
    pieces, events = plan(rows, width, sizes)
    nocc = nz * nx

    def device(dx, dy, dz, dc):
        return (
            ((z + turn * dz + nz) % nz) * nx + (x + dx + nx) % nx,
            ((y + dy + ny) % ny) * CORES + (core + dc) % CORES,
        )

    barrier = pltpu.get_barrier_semaphore()
    for step in range(1, nocc):
        pl.semaphore_signal(barrier, inc=1, device_id=((occ + step) % nocc, aux), device_id_type=MESH)
    near = [(occ, (aux // CORES) * CORES + (core + 1) % CORES)]
    for way in (1, -1):
        if reach(ny)[way] >= 1:
            near.append(device(0, way, 0, 0))
    for target in near:
        pl.semaphore_signal(barrier, inc=1, device_id=target, device_id_type=MESH)
    pl.semaphore_wait(barrier, nocc - 1 + len(near))

    def columns(shard_aux):
        return pl.ds(pl.multiple_of(shard_aux * width, width), width)

    def place(at, shard):
        low, number, _ = pieces[at]
        return blocks.at[shard[0], pl.ds(low, number), columns(shard[1])]

    def source(at, shard, own):
        low, number, _ = pieces[at]
        return b_ref.at[pl.ds(low, number)] if own else place(at, shard)

    own_copy = pltpu.make_async_copy(b_ref, blocks.at[occ, :, columns(aux)], own_sem)
    own_copy.start()
    sent = []

    def send(at, shard, own, target):
        copy = pltpu.make_async_remote_copy(
            src_ref=source(at, shard, own), dst_ref=place(at, shard),
            send_sem=send_sem.at[len(sent)], recv_sem=recv_sem.at[at, shard[0], shard[1]],
            device_id=target, device_id_type=MESH,
        )
        copy.start()
        sent.append(copy)

    def arrive(at, shard):
        spot = place(at, shard)
        pltpu.make_async_remote_copy(
            src_ref=spot, dst_ref=spot, send_sem=own_sem, recv_sem=recv_sem.at[at, shard[0], shard[1]],
            device_id=(occ, aux), device_id_type=MESH,
        ).wait_recv()

    left = {}
    ready = []
    for _, at, rel, kind, _ in events:
        key = (rel[0] % nx, rel[2] % nz)
        left[key] = left.get(key, 0) + 1
    waiting = {"energies": True}
    small = []
    done = [False]

    def compute(key):
        block = device(-key[0], 0, -key[1], 0)[0]
        mine, other = blocks.at[occ], blocks.at[block]
        value = lax.dot_general(mine[...], other[...], (((1,), (1,)), ((), ())), preferred_element_type=jnp.float32)
        numer = 2.0 * value - value.T
        denom = col_ref[...] + row_ref[...] - e_ref[0:1, 0:1] - energies[block, 0:1, 0:1]
        amps = (numer / denom).astype(jnp.bfloat16)
        term = jnp.dot(amps, blocks[block, :, columns(aux)], preferred_element_type=jnp.float32)
        out_ref[...] = out_ref[...] + term if done[0] else term
        done[0] = True

    started = False
    for _, at, rel, kind, sends in events:
        dx, dy, dz = -rel[0], -rel[1], -rel[2]
        key = (rel[0] % nx, rel[2] % nz)
        if kind == "core":
            arrive(at, partner_shard(device, nz, nx, z, x, y, core, turn, dx, dy, dz, ny))
            rel_key = (rel[0] % nx, (-rel[2]) % nz)
            key = rel_key
        else:
            shard = device(dx, dy, dz, 0)
            if kind == "link":
                arrive(at, shard)
            for dim, way in sends:
                step = {"x": 0, "y": 0, "z": 0}
                step[dim] = way
                send(at, shard, kind == "own", device(step["x"], step["y"], step["z"], 0))
            send(at, shard, kind == "own", device(0, 0, 0, 1))
        left[key] -= 1
        if kind == "own" and not started and at == len(pieces) - 1:
            started = True
            keep = pltpu.make_async_copy(e_ref, energies.at[occ], esend_sem.at[0])
            keep.start()
            for step in range(1, nocc):
                copy = pltpu.make_async_remote_copy(
                    src_ref=e_ref, dst_ref=energies.at[occ], send_sem=esend_sem.at[step],
                    recv_sem=erecv_sem.at[occ], device_id=((occ + step) % nocc, aux), device_id_type=MESH,
                )
                copy.start()
                small.append(copy)
            keep.wait()
            own_copy.wait()
        if left[key] == 0:
            left[key] = -1
            ready.append(key)
            if (0, 0) in ready or done[0]:
                for one in ready:
                    if one != (0, 0) and waiting["energies"]:
                        waiting["energies"] = False
                        for step in range(1, nocc):
                            who = (occ + step) % nocc
                            pltpu.make_async_remote_copy(
                                src_ref=e_ref, dst_ref=energies.at[who], send_sem=own_sem,
                                recv_sem=erecv_sem.at[who], device_id=(occ, aux), device_id_type=MESH,
                            ).wait_recv()
                    compute(one)
                ready.clear()
    for copy in sent + small:
        copy.wait_send()


def partner_shard(device, nz, nx, z, x, y, core, turn, dx, dy, dz, ny):
    return (
        ((z - turn * dz + nz) % nz) * nx + (x + dx + nx) % nx,
        ((y + dy + ny) % ny) * CORES + (core + 1) % CORES,
    )


def gathered(three_index, occ_energy, vir_energy, nz, nx, ny):
    _, rows, width = three_index.shape
    nocc, naux = nz * nx, ny * CORES
    pieces, events = plan(rows, width, {"x": nx, "y": ny, "z": nz})
    copies = sum(len(e[4]) + 1 for e in events if e[3] != "core")
    energy = jnp.broadcast_to(occ_energy.reshape(1, 1), (8, 128))
    vmem = pl.BlockSpec(memory_space=pltpu.VMEM)
    out = pl.pallas_call(
        functools.partial(gather_kernel, nz, nx, ny),
        out_shape=jax.ShapeDtypeStruct((rows, width), jnp.float32),
        in_specs=[vmem] * 4,
        out_specs=vmem,
        scratch_shapes=[
            pltpu.VMEM((nocc, rows, naux * width), three_index.dtype),
            pltpu.VMEM((nocc, 8, 128), jnp.float32),
            pltpu.SemaphoreType.DMA((copies,)),
            pltpu.SemaphoreType.DMA((len(pieces), nocc, naux)),
            pltpu.SemaphoreType.DMA((nocc,)),
            pltpu.SemaphoreType.DMA((nocc,)),
            pltpu.SemaphoreType.DMA,
        ],
        compiler_params=pltpu.CompilerParams(
            collective_id=0, has_side_effects=True, vmem_limit_bytes=48 * 1024 * 1024
        ),
    )(three_index[0], energy, vir_energy[:, None], vir_energy[None, :])
    return out[None]


def pair_amps(rows_i, eps_i, rows_j, eps_j, vir_energy):
    partial_value = lax.dot_general(
        rows_i, rows_j, (((1,), (1,)), ((), ())), preferred_element_type=jnp.float32
    )
    occ_count = eps_i.shape[0]
    vir_count = vir_energy.shape[0]
    width = occ_count * vir_count
    four = partial_value.reshape(occ_count, vir_count, occ_count, vir_count)
    numer = (2.0 * four - jnp.transpose(four, (0, 3, 2, 1))).reshape(width, width)
    denom = (
        vir_energy[None, :, None, None]
        + vir_energy[None, None, None, :]
        - eps_i[:, None, None, None]
        - eps_j[None, None, :, None]
    ).reshape(width, width)
    share = width // lax.axis_size("aux")
    mine = lax.psum_scatter(numer, "aux", scatter_dimension=0, tiled=True)
    lower = lax.axis_index("aux") * share
    denom_rows = lax.dynamic_slice_in_dim(denom, lower, share, 0)
    amps_rows = (mine / denom_rows).astype(jnp.bfloat16)
    amps = lax.all_gather(amps_rows, "aux", axis=0, tiled=True)
    return amps


def apply_other(amps, rows_i):
    return lax.dot_general(
        amps, rows_i, (((0,), (0,)), ((), ())), preferred_element_type=jnp.float32
    )


def local(three_index, occ_energy, vir_energy):
    occ_count, vir_count, aux_count = three_index.shape
    cycle_size = lax.axis_size("occ")
    my_index = lax.axis_index("occ")
    all_energy = lax.all_gather(occ_energy, "occ", axis=0, tiled=True)
    own_rows = three_index.reshape(occ_count * vir_count, aux_count)

    def energy_of(step):
        block = (my_index - step + cycle_size) % cycle_size
        return lax.dynamic_slice_in_dim(all_energy, block * occ_count, occ_count)

    amps = pair_amps(own_rows, occ_energy, own_rows, occ_energy, vir_energy)
    gamma = jnp.dot(amps, own_rows, preferred_element_type=jnp.float32)
    half = cycle_size // 2
    carried = jnp.zeros_like(gamma)

    def cycle_step(step, state):
        rows_j, carried, gamma = state
        rows_j = from_behind(rows_j, "occ", 1)
        carried = from_behind(carried, "occ", 1)
        amps = pair_amps(own_rows, occ_energy, rows_j, energy_of(step), vir_energy)
        gamma = gamma + jnp.dot(amps, rows_j, preferred_element_type=jnp.float32)
        carried = carried + apply_other(amps, own_rows)
        return (rows_j, carried, gamma)

    rows_j, carried, gamma = lax.fori_loop(1, half, cycle_step, (own_rows, carried, gamma))
    rows_j = from_behind(rows_j, "occ", 1)
    amps = pair_amps(own_rows, occ_energy, rows_j, energy_of(half), vir_energy)
    gamma = gamma + jnp.dot(amps, rows_j, preferred_element_type=jnp.float32)
    returned = from_behind(carried, "occ", 1 - half)
    gamma = gamma + returned
    return gamma.reshape(occ_count, vir_count, aux_count)


def solution(mesh):
    nocc, naux = mesh.shape["occ"], mesh.shape["aux"]

    def either(three_index, occ_energy, vir_energy):
        _, rows, width = three_index.shape
        whole = nocc * naux * three_index.size * three_index.dtype.itemsize
        fits = whole <= GATHER_LIMIT and three_index.shape[0] == 1
        if fits and naux % CORES == 0 and nocc % 2 == 0:
            return gathered(three_index, occ_energy, vir_energy, nocc // 2, 2, naux // CORES)
        return local(three_index, occ_energy, vir_energy)

    return jax.shard_map(
        either,
        mesh=mesh,
        in_specs=(P("occ", None, "aux"), P("occ"), P()),
        out_specs=P("occ", None, "aux"),
        check_vma=False,
    )
```

profile of v0, /device:TPU:0, one launch (start us, length us, event | category | flops | bytes accessed | tf_op | source)
XLA Modules:
  0.0 57.8 jit_solution(6347712836283789635)
XLA Ops:
  0.7 0.0 copy-start.1
  0.7 0.7 %copy-done.1 = f32[448]{0:T(512)S(1)} copy-done((f32[448]{0:T(512)S(1)}, f32[448]{0:T(512)}, u32[]{:S(2)}) %copy-start.1) | copy-done | bytes 1816
  1.3 0.1 copy.4.col_ref
  1.5 0.0 copy-start
  1.5 1.0 %copy-done = bf16[1,448,384]{2,1,0:T(8,128)(2,1)S(1)} copy-done((bf16[1,448,384]{2,1,0:T(8,128)(2,1)S(1)}, bf16[1,448,384]{2,1,0:T(8,128)(2,1)}, u32[]{:S(2)}) %copy-start) | copy-done | bytes 344088
  2.5 54.5 %shard_map.37 = f32[448,384]{1,0:T(8,128)S(1)} custom-call(bf16[448,384]{1,0:T(8,128)(2,1)S(1)} %bitcast.7, f32[8,128]{1,0:T(8,128)S(1)} %broadcast_in_dim.17.e_ref, f32[448,1]{1,0:T(8,128)S(1)} %copy.4.col_ref, f32[1,448]{1,0:T(1,128)S(1)} %bitcast.9), custom_call_target="tpu_custom_call" | custom-call | tf_op jit(solution)/shard_map/pallas_call | solution.py:236
  57.0 0.8 %copy.7 = f32[1,448,384]{2,1,0:T(8,128)} copy(f32[1,448,384]{2,1,0:T(8,128)S(1)} %bitcast.6) | data formatting | bytes 1376256
  (1 shorter events, 0.0 us)
Async XLA Ops:
  0.7 0.7 %copy-start.1 = (f32[448]{0:T(512)S(1)}, f32[448]{0:T(512)}, u32[]{:S(2)}) copy-start(f32[448]{0:T(512)} %param.5) | copy-start | bytes 5380
  1.5 1.0 %copy-start = (bf16[1,448,384]{2,1,0:T(8,128)(2,1)S(1)}, bf16[1,448,384]{2,1,0:T(8,128)(2,1)}, u32[]{:S(2)}) copy-start(bf16[1,448,384]{2,1,0:T(8,128)(2,1)} %param.3) | copy-start | bytes 1032196
where the time goes:
time: 58.9 us; the launch traced here: 57.8 us
  Pallas kernels  54.5 us (93%)
  local copies, waits for them, and re-layouts  2.63 us (4%)
  between operations  0.69 us (1%)
    pallas_call x1, Pallas kernels, gathered(): pl.pallas_call(functools.partial(gather_kernel, nz, nx, ny), out_shape=ja...  54.5 us
    unnamed x5, local copies, waits for them, and re-layouts  2.49 us

commit v1 on v0

--- a/solution.py
+++ b/solution.py
@@ -11,8 +11,8 @@
 MESH = pl.DeviceIdType.MESH
 CORES = 2
 GATHER_LIMIT = 24 * 1024 * 1024
-PIECES = ((0.145, "yxz"), (0.43, "zyx"), (0.43, "zxy"))
-RATE = {"x": 46.0, "y": 46.0, "z": 25.0, "c": 150.0}
+PIECES = ((0.25, "yxz"), (0.25, "xyz"), (0.25, "zyx"), (0.25, "zxy"))
+RATE = {"x": 46.0, "y": 46.0, "z": 46.0, "c": 500.0}
 HOP = {"x": 1700.0, "y": 1700.0, "z": 1700.0, "c": 900.0}
 
 

time: 58.9 us -> 78.8 us (1.34)
  Pallas kernels: 54.5 us -> 74.6 us
    pallas_call x1, Pallas kernels: 54.5 us -> 74.6 us  [gathered(): pl.pallas_call(functools.partial(gather_kernel, nz, nx, ny), out_shape=ja...]
where the time goes in v1:
time: 78.8 us; the launch traced here: 77.9 us
  Pallas kernels  74.6 us (95%)
  local copies, waits for them, and re-layouts  2.63 us (3%)
    pallas_call x1, Pallas kernels, gathered(): pl.pallas_call(functools.partial(gather_kernel, nz, nx, ny), out_shape=ja...  74.6 us
    unnamed x5, local copies, waits for them, and re-layouts  2.49 us

profile of v1, /device:TPU:0, one launch (start us, length us, event | category | flops | bytes accessed | tf_op | source)
XLA Modules:
  0.0 77.9 jit_solution(1561807327645843626)
XLA Ops:
  0.7 0.0 copy-start.1
  0.7 0.7 copy-done.1
  1.3 0.1 copy.4.col_ref
  1.5 0.0 copy-start
  1.5 1.0 %copy-done = bf16[1,448,384]{2,1,0:T(8,128)(2,1)S(1)} copy-done((bf16[1,448,384]{2,1,0:T(8,128)(2,1)S(1)}, bf16[1,448,384]{2,1,0:T(8,128)(2,1)}, u32[]{:S(2)}) %copy-start) | copy-done | bytes 344088
  2.5 74.6 %shard_map.37 = f32[448,384]{1,0:T(8,128)S(1)} custom-call(bf16[448,384]{1,0:T(8,128)(2,1)S(1)} %bitcast.7, f32[8,128]{1,0:T(8,128)S(1)} %broadcast_in_dim.17.e_ref, f32[448,1]{1,0:T(8,128)S(1)} %copy.4.col_ref, f32[1,448]{1,0:T(1,128)S(1)} %bitcast.9), custom_call_target="tpu_custom_call" | custom-call | tf_op jit(solution)/shard_map/pallas_call | solution.py:236
  77.1 0.8 %copy.7 = f32[1,448,384]{2,1,0:T(8,128)} copy(f32[1,448,384]{2,1,0:T(8,128)S(1)} %bitcast.6) | data formatting | bytes 1376256
  (1 shorter events, 0.0 us)
Async XLA Ops:
  0.7 0.7 copy-start.1
  1.5 1.0 %copy-start = (bf16[1,448,384]{2,1,0:T(8,128)(2,1)S(1)}, bf16[1,448,384]{2,1,0:T(8,128)(2,1)}, u32[]{:S(2)}) copy-start(bf16[1,448,384]{2,1,0:T(8,128)(2,1)} %param.3) | copy-start | bytes 1032196

commit v2 on v1

v2 whole, which is shorter than its diff:
```python
import functools
import heapq
import itertools

import jax
import jax.numpy as jnp
from jax import lax
from jax.experimental import pallas as pl
from jax.experimental.pallas import tpu as pltpu
from jax.sharding import PartitionSpec as P

MESH = pl.DeviceIdType.MESH
CORES = 2
GATHER_LIMIT = 24 * 1024 * 1024
LANES = 128
RATE = 46250.0
HOP = 2.4
AHEAD = 2.0
SLACK = 0.0
RETURN = 5.3
LAST = 50
MIRROR = 1.0
MATMUL = 0.45
ELEMENT = 0.25
APPLY = 0.35
EXCHANGE = 1.5
STEP = {"x": (1, 0, 0), "y": (0, 1, 0), "+": (0, 0, 1), "-": (0, 0, -1)}
BACK = {"x": "x", "y": "y", "+": "-", "-": "+"}
ROUTES = (
    (".xyxy+++x++y....", ".xyy+++x+xyx....", ".xyx+++++xy+....", ".xyx+-+++xyy...."),
    ("-yx-.xyx++yx+xyx", "-yyx.xxy+xy-x+xy", "y--y.xyy++-++xyy", "---x.yyx+x++yyx+"),
)
URGENCY = (4, -1, 0, 0, -2, -4, 0, 1)
DEPTH = 0.5


def from_behind(array, axis, by):
    size = lax.axis_size(axis)
    return lax.ppermute(array, axis, [(i, (i + by) % size) for i in range(size)])


def moved(chip, link):
    dx, dy, dz = STEP[link]
    return ((chip[0] + dx) % 2, (chip[1] + dy) % 2, chip[2] + dz)


def piece_rows(rows):
    number = len(ROUTES[0])
    tiles = rows // 16
    lows = [16 * (tiles * at // number) for at in range(number)] + [rows]
    return [(lows[at], lows[at + 1] - lows[at]) for at in range(number)]


def routes():
    out = []
    for a, b, mirrored in itertools.product(range(2), repeat=3):
        for plane in range(2):
            for piece, text in enumerate(ROUTES[plane]):
                tree = {}
                for z, y, x in itertools.product(range(4), range(2), range(2)):
                    link = text[x + 2 * y + 4 * z]
                    if link == ".":
                        continue
                    px, py, pz = moved((x, y, z), BACK[link])
                    parent = (px ^ a, py ^ b, 3 - pz if mirrored else pz)
                    tree.setdefault(parent, []).append(BACK[link] if mirrored and link in "+-" else link)
                out.append(((a, b, 3 - plane if mirrored else plane), piece, tree))
    return out


def depth_of(tree, chip, known):
    if chip not in known:
        known[chip] = 1 + max([depth_of(tree, moved(chip, link), known) for link in tree.get(chip, ())] or [-1])
    return known[chip]


def timeline(pieces, width):
    items = routes()
    known = [{} for _ in items]
    waiting, busy, arrivals, order, heap = {}, set(), {}, {}, []
    plain = len(items)
    missing = {(x, y, z): 4 * len(pieces) for x, y, z in itertools.product(range(2), range(2), (1, 2))}
    count = itertools.count()
    for at, (source, _, _) in enumerate(items):
        heapq.heappush(heap, (0.0, next(count), True, at, source))

    def start(lane, now):
        if lane in busy or not waiting.get(lane):
            return
        _, _, at, target = heapq.heappop(waiting[lane])
        busy.add(lane)
        taken = pieces[items[at][1]][1] * width * 2 / RATE
        order.setdefault(lane, []).append((now, at))
        heapq.heappush(heap, (now + taken, next(count), False, lane, None))
        heapq.heappush(heap, (now + taken + HOP, next(count), True, at, target))

    while heap:
        now, _, arrived, at, chip = heapq.heappop(heap)
        if not arrived:
            busy.discard(at)
            start(at, now)
            continue
        source, _, tree = items[at]
        arrivals[at, chip] = now
        if at < plain and chip in missing and source[2] == (3 if chip[2] == 1 else 0):
            missing[chip] -= 1
            if missing[chip] == 0:
                for piece in range(len(pieces)):
                    items.append((chip, piece, {chip: ["-" if chip[2] == 1 else "+"]}))
                    known.append({})
                    heapq.heappush(heap, (now + RETURN, next(count), True, len(items) - 1, chip))
        for link in tree.get(chip, ()):
            target = moved(chip, link)
            plane, goal = source[2], target[2]
            if goal >= 2:
                plane, goal = 3 - plane, 3 - goal
            rank = -DEPTH * depth_of(tree, target, known[at]) - URGENCY[2 * plane + goal] if at < plain else LAST
            heapq.heappush(waiting.setdefault((chip, link), []), (rank, next(count), at, target))
            start((chip, link), now)
    return items, arrivals, order, plain


def compute_steps(ready, inner):
    own = 1 if inner else 0
    tasks = []
    for plane, when in ready.items():
        if inner and plane == 3:
            tasks.append((max(when, ready[0]), 0, plane, True))
        tasks.append((max(when, ready[own]), 1, plane, False))
    tasks.sort()
    steps, clock, later = [], 0.0, []
    halves, parts = 2, 4

    def settle(now):
        nonlocal clock
        while later and later[0][0] <= now:
            when, at = heapq.heappop(later)
            clock = max(clock, when)
            steps.append((clock, "other", at, 0))
            clock += APPLY
            if tasks[at][3]:
                steps.append((clock, "return", at, 0))

    for at, (when, _, plane, far) in enumerate(tasks):
        settle(max(clock, when))
        clock = max(clock, when)
        steps.append((clock, "open", at, 0))
        for part in range(halves):
            settle(clock)
            steps.append((clock, "matmul", at, part))
            clock += MATMUL
        for part in range(parts):
            settle(clock)
            steps.append((clock, "element", at, part))
            clock += ELEMENT
        steps.append((clock, "mine", at, 0))
        clock += APPLY
        heapq.heappush(later, (clock + EXCHANGE, at))
    settle(1e9)
    return [(plane, far) for _, _, plane, far in tasks], steps, clock


def program_of(plane, pieces, width):
    items, arrivals, order, plain = timeline(pieces, width)
    chip = (0, 0, plane)
    events = []
    ready = {}
    for at, (source, piece, _) in enumerate(items[:plain]):
        if (at, chip) in arrivals:
            ready[source[2]] = max(ready.get(source[2], 0.0), arrivals[at, chip] + MIRROR)
    tasks, steps, end = compute_steps(ready, plane == 1)
    back = max([when for when, kind, _, _ in steps if kind == "return"] or [0.0])
    first = {}
    for link in STEP:
        last = 0.0
        for when, at in order.get((chip, link), ()):
            last = max(last, arrivals[at, chip], when - AHEAD)
            if at < plain:
                first[at] = min(first.get(at, 1e9), last)
                events.append((last, 2, ("send", items[at][0], items[at][1], link)))
            else:
                events.append((max(last, back + 0.01), 4, ("return", items[at][1])))
    for at, (source, piece, _) in enumerate(items[:plain]):
        if (at, chip) in arrivals:
            when = min(arrivals[at, chip] + SLACK, first.get(at, 1e9))
            events.append((when, 1, ("take", source, piece)))
    events += [(when, 3, ("step", *step)) for when, *step in steps]
    for away in range(4 if plane == 1 else 3):
        if away != plane:
            events.append((5.0 * abs(away - plane), 0, ("energy", away)))
    if plane == 0:
        events.append((end + 100.0, 4, ("far",)))
    events.sort(key=lambda event: event[:2])
    return [event[2] for event in events], tasks


def gather_kernel(nz, nx, ny, b_ref, e_ref, col_ref, row_ref, out_ref, blocks, energies, value, mine_amps, other_amps,
                  total, leave, come, send_sem, recv_sem, msend_sem, mrecv_sem, esend_sem, erecv_sem,
                  asend_sem, arecv_sem, fsend_sem, frecv_sem, unused_sem):
    rows, width = b_ref.shape
    occ, aux = lax.axis_index("occ"), lax.axis_index("aux")
    z, x = occ // nx, occ % nx
    y, core = aux // CORES, aux % CORES
    upper = z // 2
    plane = z + upper * (nz - 1 - 2 * z)
    pieces = piece_rows(rows)

    def plane_at(k):
        return k + upper * (nz - 1 - 2 * k)

    def block_at(dx, k):
        return plane_at(k) * nx + (x + dx) % nx

    def device(dx, dy, k, dc=0):
        return block_at(dx, k), ((y + dy) % ny) * CORES + (core + dc) % CORES

    def neighbour(me, link):
        dx, dy, dz = STEP[link]
        return device(dx, dy, me + dz)

    partner = (occ, y * CORES + (core + 1) % CORES)
    barrier = pltpu.get_barrier_semaphore()
    step_up = 1 - 2 * upper
    near = [
        partner,
        (z * nx + (x + 1) % nx, aux),
        (occ, ((y + 1) % ny) * CORES + core),
        ((z + step_up) * nx + x, aux),
    ]
    for target in near:
        pl.semaphore_signal(barrier, inc=1, device_id=target, device_id_type=MESH)

    @pl.when(plane == 1)
    def _():
        pl.semaphore_signal(barrier, inc=1, device_id=((z - step_up) * nx + x, aux), device_id_type=MESH)

    pl.semaphore_wait(barrier, len(near) + plane)

    def columns(shard_aux):
        return pl.ds(pl.multiple_of(shard_aux * width, width), width)

    def run(me):
        events, tasks = program_of(me, pieces, width)
        sent = []
        taken = set()
        started = {}

        def place(source, piece, dc=0):
            block, shard_aux = device(source[0], source[1], source[2], dc)
            low, number = pieces[piece]
            return blocks.at[block, pl.ds(low, number), columns(shard_aux)]

        def chip_index(source):
            block, shard_aux = device(*source)
            return block * ny + shard_aux // CORES

        def origin(source, piece):
            low, number = pieces[piece]
            return b_ref.at[pl.ds(low, number)] if source == (0, 0, me) else place(source, piece)

        def remote(src, dst, send, recv, target):
            return pltpu.make_async_remote_copy(
                src_ref=src, dst_ref=dst, send_sem=send, recv_sem=recv, device_id=target, device_id_type=MESH
            )

        def start(copy):
            copy.start()
            sent.append(copy)

        def arrived(spot, sem):
            remote(spot, spot, unused_sem, sem, (occ, aux)).wait_recv()

        for target in ["x", "+"] + (["-"] if me == 1 else []):
            start(remote(e_ref, energies.at[occ], esend_sem.at[len(sent)], erecv_sem.at[occ], neighbour(me, target)))
        number_sent = [0]

        def send(source, piece, link):
            copy = remote(
                origin(source, piece), place(source, piece), send_sem.at[number_sent[0]],
                recv_sem.at[piece, chip_index(source)], neighbour(me, link),
            )
            number_sent[0] += 1
            start(copy)

        def take(source, piece):
            if source != (0, 0, me):
                arrived(place(source, piece), recv_sem.at[piece, chip_index(source)])
            start(remote(
                origin(source, piece), place(source, piece), msend_sem.at[piece, chip_index(source)],
                mrecv_sem.at[piece, chip_index(source)], partner,
            ))

        def pass_energy(away):
            if away in passed:
                return
            passed.add(away)
            block = block_at(0, away)
            arrived(energies.at[block], erecv_sem.at[block])
            onward = ["x"] + ({0: ["+"], 2: ["-"]}.get(away, []) if me == 1 else [])
            for link in onward:
                start(remote(energies.at[block], energies.at[block], esend_sem.at[count_energy[0]],
                             erecv_sem.at[block], neighbour(me, link)))
                count_energy[0] += 1

        count_energy = [len(sent)]
        passed = {me}
        blocks[occ, :, columns(aux)] = b_ref[...]
        energies[occ] = e_ref[...]

        def open_plane(k):
            if k in taken:
                return
            taken.add(k)
            pass_energy(k)
            for source in itertools.product(range(2), range(2), [k]):
                for piece in range(len(pieces)):
                    arrived(place(source, piece, 1), mrecv_sem.at[piece, chip_index(source)])
            block = block_at(1, k)
            arrived(energies.at[block], erecv_sem.at[block])

        def apply(amps, block, far, fresh):
            term = jnp.dot(amps, blocks[block, :, columns(aux)], preferred_element_type=jnp.float32)
            goal = total if far else out_ref
            goal[...] = term if fresh else goal[...] + term

        def step(kind, at, part):
            k, far = tasks[at]
            left = block_at(0, 0) if far else occ
            right = plane_at(k) * nx + (x + core) % nx
            if kind == "open":
                open_plane(0 if far else me)
                open_plane(k)
            elif kind == "matmul":
                cut = rows // 2 // LANES * LANES + LANES if rows > LANES else rows
                low, high = ((0, min(cut, rows)), (min(cut, rows), rows))[part]
                if high > low:
                    value[:, low:high] = lax.dot_general(
                        blocks[left], blocks[right, low:high, :], (((1,), (1,)), ((), ())),
                        preferred_element_type=jnp.float32,
                    )
            elif kind == "element":
                size = -(-rows // (4 * LANES)) * LANES
                low, high = min(part * size, rows), min(part * size + size, rows)
                if high > low:
                    numer = 2.0 * value[low:high, :] - value[:, low:high].T
                    denom = col_ref[low:high, :] + row_ref[...] - energies[left, 0:1, 0:1] - energies[right, 0:1, 0:1]
                    mine_amps[at, low:high, :] = (numer / denom).astype(jnp.bfloat16)
            elif kind == "mine":
                apply(mine_amps[at], right, far, far not in started)
                started[far] = True
                start(remote(mine_amps.at[at], other_amps.at[at], asend_sem.at[at], arecv_sem.at[at], partner))
            elif kind == "other":
                arrived(other_amps.at[at], arecv_sem.at[at])
                apply(other_amps[at], plane_at(k) * nx + (x + 1 - core) % nx, far, False)
            elif kind == "return":
                leave[...] = total[...].astype(jnp.bfloat16)

        for event in events:
            if event[0] == "take":
                take(*event[1:])
            elif event[0] == "send":
                send(*event[1:])
            elif event[0] == "energy":
                pass_energy(event[1])
            elif event[0] == "step":
                step(*event[1:])
            elif event[0] == "return":
                spot = pl.ds(*pieces[event[1]])
                start(remote(leave.at[spot], come.at[spot], fsend_sem.at[event[1]], frecv_sem.at[event[1]],
                             neighbour(me, "-")))
            else:
                for piece, (low, number) in enumerate(pieces):
                    spot = slice(low, low + number)
                    arrived(come.at[pl.ds(low, number)], frecv_sem.at[piece])
                    out_ref[spot, :] = out_ref[spot, :] + come[spot, :].astype(jnp.float32)
        for copy in sent:
            copy.wait_send()

    @pl.when(plane == 0)
    def _():
        run(0)

    @pl.when(plane == 1)
    def _():
        run(1)


def gathered(three_index, occ_energy, vir_energy, nz, nx, ny):
    _, rows, width = three_index.shape
    nocc, naux = nz * nx, ny * CORES
    pieces = piece_rows(rows)
    copies = max(sum(event[0] == "send" for event in program_of(plane, pieces, width)[0]) for plane in range(2))
    tasks = 5
    energy = jnp.broadcast_to(occ_energy.reshape(1, 1), (8, LANES))
    vmem = pl.BlockSpec(memory_space=pltpu.VMEM)
    dma = pltpu.SemaphoreType.DMA
    kind = three_index.dtype
    out = pl.pallas_call(
        functools.partial(gather_kernel, nz, nx, ny),
        out_shape=jax.ShapeDtypeStruct((rows, width), jnp.float32),
        in_specs=[vmem] * 4,
        out_specs=vmem,
        scratch_shapes=[
            pltpu.VMEM((nocc, rows, naux * width), kind),
            pltpu.VMEM((nocc, 8, LANES), jnp.float32),
            pltpu.VMEM((rows, rows), jnp.float32),
            pltpu.VMEM((tasks, rows, rows), jnp.bfloat16),
            pltpu.VMEM((tasks, rows, rows), jnp.bfloat16),
            pltpu.VMEM((rows, width), jnp.float32),
            pltpu.VMEM((rows, width), jnp.bfloat16),
            pltpu.VMEM((rows, width), jnp.bfloat16),
            dma((copies,)),
            dma((len(pieces), nocc * ny)),
            dma((len(pieces), nocc * ny)),
            dma((len(pieces), nocc * ny)),
            dma((16,)),
            dma((nocc,)),
            dma((tasks,)),
            dma((tasks,)),
            dma((len(pieces),)),
            dma((len(pieces),)),
            dma,
        ],
        compiler_params=pltpu.CompilerParams(
            collective_id=0, has_side_effects=True, vmem_limit_bytes=48 * 1024 * 1024
        ),
    )(three_index[0], energy, vir_energy[:, None], vir_energy[None, :])
    return out[None]


def pair_amps(rows_i, eps_i, rows_j, eps_j, vir_energy):
    partial_value = lax.dot_general(
        rows_i, rows_j, (((1,), (1,)), ((), ())), preferred_element_type=jnp.float32
    )
    occ_count = eps_i.shape[0]
    vir_count = vir_energy.shape[0]
    width = occ_count * vir_count
    four = partial_value.reshape(occ_count, vir_count, occ_count, vir_count)
    numer = (2.0 * four - jnp.transpose(four, (0, 3, 2, 1))).reshape(width, width)
    denom = (
        vir_energy[None, :, None, None]
        + vir_energy[None, None, None, :]
        - eps_i[:, None, None, None]
        - eps_j[None, None, :, None]
    ).reshape(width, width)
    share = width // lax.axis_size("aux")
    mine = lax.psum_scatter(numer, "aux", scatter_dimension=0, tiled=True)
    lower = lax.axis_index("aux") * share
    denom_rows = lax.dynamic_slice_in_dim(denom, lower, share, 0)
    amps_rows = (mine / denom_rows).astype(jnp.bfloat16)
    amps = lax.all_gather(amps_rows, "aux", axis=0, tiled=True)
    return amps


def apply_other(amps, rows_i):
    return lax.dot_general(
        amps, rows_i, (((0,), (0,)), ((), ())), preferred_element_type=jnp.float32
    )


def local(three_index, occ_energy, vir_energy):
    occ_count, vir_count, aux_count = three_index.shape
    cycle_size = lax.axis_size("occ")
    my_index = lax.axis_index("occ")
    all_energy = lax.all_gather(occ_energy, "occ", axis=0, tiled=True)
    own_rows = three_index.reshape(occ_count * vir_count, aux_count)

    def energy_of(step):
        block = (my_index - step + cycle_size) % cycle_size
        return lax.dynamic_slice_in_dim(all_energy, block * occ_count, occ_count)

    amps = pair_amps(own_rows, occ_energy, own_rows, occ_energy, vir_energy)
    gamma = jnp.dot(amps, own_rows, preferred_element_type=jnp.float32)
    half = cycle_size // 2
    carried = jnp.zeros_like(gamma)

    def cycle_step(step, state):
        rows_j, carried, gamma = state
        rows_j = from_behind(rows_j, "occ", 1)
        carried = from_behind(carried, "occ", 1)
        amps = pair_amps(own_rows, occ_energy, rows_j, energy_of(step), vir_energy)
        gamma = gamma + jnp.dot(amps, rows_j, preferred_element_type=jnp.float32)
        carried = carried + apply_other(amps, own_rows)
        return (rows_j, carried, gamma)

    rows_j, carried, gamma = lax.fori_loop(1, half, cycle_step, (own_rows, carried, gamma))
    rows_j = from_behind(rows_j, "occ", 1)
    amps = pair_amps(own_rows, occ_energy, rows_j, energy_of(half), vir_energy)
    gamma = gamma + jnp.dot(amps, rows_j, preferred_element_type=jnp.float32)
    returned = from_behind(carried, "occ", 1 - half)
    gamma = gamma + returned
    return gamma.reshape(occ_count, vir_count, aux_count)


def solution(mesh):
    nocc, naux = mesh.shape["occ"], mesh.shape["aux"]

    def either(three_index, occ_energy, vir_energy):
        _, rows, width = three_index.shape
        whole = nocc * naux * three_index.size * three_index.dtype.itemsize
        pieces = len(ROUTES[0])
        fits = whole <= GATHER_LIMIT and three_index.shape[0] == 1
        fits = fits and rows % 16 == 0 and rows // 16 >= pieces and width % LANES == 0
        if fits and nocc == 8 and naux == 2 * CORES:
            return gathered(three_index, occ_energy, vir_energy, nocc // 2, 2, naux // CORES)
        return local(three_index, occ_energy, vir_energy)

    return jax.shard_map(
        either,
        mesh=mesh,
        in_specs=(P("occ", None, "aux"), P("occ"), P()),
        out_specs=P("occ", None, "aux"),
        check_vma=False,
    )
```

time: 78.8 us -> 54.5 us (0.69)
  Pallas kernels: 74.6 us -> 51 us
    pallas_call x1, Pallas kernels: 74.6 us -> 51 us  [gathered(): pl.pallas_call(functools.partial(gather_kernel, nz, nx, ny), out_shape=ja...]
where the time goes in v2:
time: 54.5 us; the launch traced here: 54.4 us
  Pallas kernels  51 us (94%)
  local copies, waits for them, and re-layouts  2.63 us (5%)
  between operations  0.69 us (1%)
    pallas_call x1, Pallas kernels, gathered(): pl.pallas_call(functools.partial(gather_kernel, nz, nx, ny), out_shape=ja...  51 us
    unnamed x5, local copies, waits for them, and re-layouts  2.49 us

profile of v2, /device:TPU:0, one launch (start us, length us, event | category | flops | bytes accessed | tf_op | source)
XLA Modules:
  0.0 54.4 jit_solution(11236126356952142681)
XLA Ops:
  0.7 0.0 copy-start.1
  0.7 0.7 %copy-done.1 = f32[448]{0:T(512)S(1)} copy-done((f32[448]{0:T(512)S(1)}, f32[448]{0:T(512)}, u32[]{:S(2)}) %copy-start.1) | copy-done | bytes 1816
  1.3 0.1 copy.4.col_ref
  1.5 0.0 copy-start
  1.5 1.0 %copy-done = bf16[1,448,384]{2,1,0:T(8,128)(2,1)S(1)} copy-done((bf16[1,448,384]{2,1,0:T(8,128)(2,1)S(1)}, bf16[1,448,384]{2,1,0:T(8,128)(2,1)}, u32[]{:S(2)}) %copy-start) | copy-done | bytes 344088
  2.5 51.0 %shard_map.37 = f32[448,384]{1,0:T(8,128)S(1)} custom-call(bf16[448,384]{1,0:T(8,128)(2,1)S(1)} %bitcast.7, f32[8,128]{1,0:T(8,128)S(1)} %broadcast_in_dim.17.e_ref, f32[448,1]{1,0:T(8,128)S(1)} %copy.4.col_ref, f32[1,448]{1,0:T(1,128)S(1)} %bitcast.9), custom_call_target="tpu_custom_call" | custom-call | tf_op jit(solution)/shard_map/pallas_call | solution.py:398
  53.5 0.8 %copy.7 = f32[1,448,384]{2,1,0:T(8,128)} copy(f32[1,448,384]{2,1,0:T(8,128)S(1)} %bitcast.6) | data formatting | bytes 1376256
  (1 shorter events, 0.0 us)
Async XLA Ops:
  0.7 0.7 %copy-start.1 = (f32[448]{0:T(512)S(1)}, f32[448]{0:T(512)}, u32[]{:S(2)}) copy-start(f32[448]{0:T(512)} %param.5) | copy-start | bytes 5380
  1.5 1.0 %copy-start = (bf16[1,448,384]{2,1,0:T(8,128)(2,1)S(1)}, bf16[1,448,384]{2,1,0:T(8,128)(2,1)}, u32[]{:S(2)}) copy-start(bf16[1,448,384]{2,1,0:T(8,128)(2,1)} %param.3) | copy-start | bytes 1032196

commit v3 on v2

--- a/solution.py
+++ b/solution.py
@@ -17,8 +17,8 @@
 HOP = 2.4
 AHEAD = 2.0
 SLACK = 0.0
-RETURN = 5.3
-LAST = 50
+RETURN = 5.0
+LAST = 0
 MIRROR = 1.0
 MATMUL = 0.45
 ELEMENT = 0.25
@@ -27,10 +27,10 @@
 STEP = {"x": (1, 0, 0), "y": (0, 1, 0), "+": (0, 0, 1), "-": (0, 0, -1)}
 BACK = {"x": "x", "y": "y", "+": "-", "-": "+"}
 ROUTES = (
-    (".xyxy+++x++y....", ".xyy+++x+xyx....", ".xyx+++++xy+....", ".xyx+-+++xyy...."),
-    ("-yx-.xyx++yx+xyx", "-yyx.xxy+xy-x+xy", "y--y.xyy++-++xyy", "---x.yyx+x++yyx+"),
+    (".xyx+x+++xyy....", ".xyx+++-+++x....", ".xyx+xy++xyy....", ".xyy+-y++xy+...."),
+    ("--yy.x+++xyyyy+x", "--yx.xyxx++-++xy", "yx-x.xy++xy-+x+y", "--yx.xyy+xy++xyx"),
 )
-URGENCY = (4, -1, 0, 0, -2, -4, 0, 1)
+URGENCY = (4, 1, -1, -2, -1, -2, -1, -1)
 DEPTH = 0.5
 
 
@@ -79,7 +79,7 @@
     known = [{} for _ in items]
     waiting, busy, arrivals, order, heap = {}, set(), {}, {}, []
     plain = len(items)
-    missing = {(x, y, z): 4 * len(pieces) for x, y, z in itertools.product(range(2), range(2), (1, 2))}
+    missing = {(x, y, z): 6 * len(pieces) for x, y, z in itertools.product(range(2), range(2), (1, 2))}
     count = itertools.count()
     for at, (source, _, _) in enumerate(items):
         heapq.heappush(heap, (0.0, next(count), True, at, source))
@@ -102,9 +102,14 @@
             continue
         source, _, tree = items[at]
         arrivals[at, chip] = now
-        if at < plain and chip in missing and source[2] == (3 if chip[2] == 1 else 0):
-            missing[chip] -= 1
-            if missing[chip] == 0:
+        if at < plain and chip in missing:
+            far, near = (3, 0) if chip[2] == 1 else (0, 3)
+            if source[2] == far or source[::2] == (chip[0], near):
+                missing[chip] -= 1
+                ended = missing[chip] == 0
+            else:
+                ended = False
+            if ended:
                 for piece in range(len(pieces)):
                     items.append((chip, piece, {chip: ["-" if chip[2] == 1 else "+"]}))
                     known.append({})
@@ -122,42 +127,29 @@
 
 def compute_steps(ready, inner):
     own = 1 if inner else 0
-    tasks = []
-    for plane, when in ready.items():
+    tasks, jobs = [], []
+    work = [("open", 0, 0.0)] + [("matmul", part, MATMUL) for part in range(2)]
+    work += [("element", part, ELEMENT) for part in range(4)] + [("mine", 0, APPLY)]
+    for plane in sorted({key[0] for key in ready}):
+        both = max(ready[plane, 0], ready[plane, 1])
         if inner and plane == 3:
-            tasks.append((max(when, ready[0]), 0, plane, True))
-        tasks.append((max(when, ready[own]), 1, plane, False))
-    tasks.sort()
-    steps, clock, later = [], 0.0, []
-    halves, parts = 2, 4
-
-    def settle(now):
-        nonlocal clock
-        while later and later[0][0] <= now:
-            when, at = heapq.heappop(later)
-            clock = max(clock, when)
-            steps.append((clock, "other", at, 0))
-            clock += APPLY
-            if tasks[at][3]:
-                steps.append((clock, "return", at, 0))
-
-    for at, (when, _, plane, far) in enumerate(tasks):
-        settle(max(clock, when))
-        clock = max(clock, when)
-        steps.append((clock, "open", at, 0))
-        for part in range(halves):
-            settle(clock)
-            steps.append((clock, "matmul", at, part))
-            clock += MATMUL
-        for part in range(parts):
-            settle(clock)
-            steps.append((clock, "element", at, part))
-            clock += ELEMENT
-        steps.append((clock, "mine", at, 0))
-        clock += APPLY
-        heapq.heappush(later, (clock + EXCHANGE, at))
-    settle(1e9)
-    return [(plane, far) for _, _, plane, far in tasks], steps, clock
+            jobs.append((max(both, ready[0, 0]), 0, len(tasks), list(work)))
+            tasks.append((plane, True))
+        jobs.append((max(both, ready[own, 0]), 2, len(tasks), list(work)))
+        tasks.append((plane, False))
+    steps, clock = [], 0.0
+    while jobs:
+        clock = max(clock, min(job[0] for job in jobs))
+        job = min((job for job in jobs if job[0] <= clock), key=lambda job: (job[1], job[0], job[2]))
+        kind, part, cost = job[3].pop(0)
+        steps.append((clock, kind, job[2], part))
+        clock += cost
+        if not job[3]:
+            jobs.remove(job)
+        if kind == "mine":
+            rest = [("other", 0, APPLY)] + ([("return", 0, 0.1)] if tasks[job[2]][1] else [])
+            jobs.append((clock + EXCHANGE, min(job[1], 1), job[2], rest))
+    return tasks, steps, clock
 
 
 def program_of(plane, pieces, width):
@@ -167,7 +159,8 @@
     ready = {}
     for at, (source, piece, _) in enumerate(items[:plain]):
         if (at, chip) in arrivals:
-            ready[source[2]] = max(ready.get(source[2], 0.0), arrivals[at, chip] + MIRROR)
+            key = (source[2], source[0])
+            ready[key] = max(ready.get(key, 0.0), arrivals[at, chip] + MIRROR)
     tasks, steps, end = compute_steps(ready, plane == 1)
     back = max([when for when, kind, _, _ in steps if kind == "return"] or [0.0])
     first = {}
@@ -196,7 +189,7 @@
 
 def gather_kernel(nz, nx, ny, b_ref, e_ref, col_ref, row_ref, out_ref, blocks, energies, value, mine_amps, other_amps,
                   total, leave, come, send_sem, recv_sem, msend_sem, mrecv_sem, esend_sem, erecv_sem,
-                  asend_sem, arecv_sem, fsend_sem, frecv_sem, unused_sem):
+                  asend_sem, arecv_sem, fsend_sem, frecv_sem, keep_sem, unused_sem):
     rows, width = b_ref.shape
     occ, aux = lax.axis_index("occ"), lax.axis_index("aux")
     z, x = occ // nx, occ % nx
@@ -218,6 +211,11 @@
         dx, dy, dz = STEP[link]
         return device(dx, dy, me + dz)
 
+    def columns(shard_aux):
+        return pl.ds(pl.multiple_of(shard_aux * width, width), width)
+
+    keep = pltpu.make_async_copy(b_ref, blocks.at[occ, :, columns(aux)], keep_sem)
+    keep.start()
     partner = (occ, y * CORES + (core + 1) % CORES)
     barrier = pltpu.get_barrier_semaphore()
     step_up = 1 - 2 * upper
@@ -236,9 +234,6 @@
 
     pl.semaphore_wait(barrier, len(near) + plane)
 
-    def columns(shard_aux):
-        return pl.ds(pl.multiple_of(shard_aux * width, width), width)
-
     def run(me):
         events, tasks = program_of(me, pieces, width)
         sent = []
@@ -304,19 +299,30 @@
 
         count_energy = [len(sent)]
         passed = {me}
-        blocks[occ, :, columns(aux)] = b_ref[...]
         energies[occ] = e_ref[...]
 
-        def open_plane(k):
-            if k in taken:
+        def open_block(dx, k):
+            if (dx, k) in taken:
                 return
-            taken.add(k)
-            pass_energy(k)
-            for source in itertools.product(range(2), range(2), [k]):
+            taken.add((dx, k))
+            if dx == 0:
+                pass_energy(k)
+            else:
+                block = block_at(1, k)
+                arrived(energies.at[block], erecv_sem.at[block])
+            if (dx, k) == (0, me):
+                keep.wait()
+            for source in itertools.product([dx], range(2), [k]):
                 for piece in range(len(pieces)):
                     arrived(place(source, piece, 1), mrecv_sem.at[piece, chip_index(source)])
-            block = block_at(1, k)
-            arrived(energies.at[block], erecv_sem.at[block])
+
+        def hand_over(at, part):
+            size = -(-rows // (4 * LANES)) * LANES
+            low, high = min(part * size, rows), min(part * size + size, rows)
+            if high > low:
+                spot = pl.ds(low, high - low)
+                start(remote(mine_amps.at[at, spot], other_amps.at[at, spot], asend_sem.at[at, part],
+                             arecv_sem.at[at, part], partner))
 
         def apply(amps, block, far, fresh):
             term = jnp.dot(amps, blocks[block, :, columns(aux)], preferred_element_type=jnp.float32)
@@ -328,13 +334,14 @@
             left = block_at(0, 0) if far else occ
             right = plane_at(k) * nx + (x + core) % nx
             if kind == "open":
-                open_plane(0 if far else me)
-                open_plane(k)
+                open_block(0, 0 if far else me)
+                open_block(0, k)
+                open_block(1, k)
             elif kind == "matmul":
                 cut = rows // 2 // LANES * LANES + LANES if rows > LANES else rows
                 low, high = ((0, min(cut, rows)), (min(cut, rows), rows))[part]
                 if high > low:
-                    value[:, low:high] = lax.dot_general(
+                    value[int(far), :, low:high] = lax.dot_general(
                         blocks[left], blocks[right, low:high, :], (((1,), (1,)), ((), ())),
                         preferred_element_type=jnp.float32,
                     )
@@ -342,15 +349,21 @@
                 size = -(-rows // (4 * LANES)) * LANES
                 low, high = min(part * size, rows), min(part * size + size, rows)
                 if high > low:
-                    numer = 2.0 * value[low:high, :] - value[:, low:high].T
+                    numer = 2.0 * value[int(far), low:high, :] - value[int(far), :, low:high].T
                     denom = col_ref[low:high, :] + row_ref[...] - energies[left, 0:1, 0:1] - energies[right, 0:1, 0:1]
                     mine_amps[at, low:high, :] = (numer / denom).astype(jnp.bfloat16)
+                if part:
+                    hand_over(at, part - 1)
             elif kind == "mine":
                 apply(mine_amps[at], right, far, far not in started)
                 started[far] = True
-                start(remote(mine_amps.at[at], other_amps.at[at], asend_sem.at[at], arecv_sem.at[at], partner))
+                hand_over(at, 3)
             elif kind == "other":
-                arrived(other_amps.at[at], arecv_sem.at[at])
+                size = -(-rows // (4 * LANES)) * LANES
+                for piece in range(4):
+                    low, high = min(piece * size, rows), min(piece * size + size, rows)
+                    if high > low:
+                        arrived(other_amps.at[at, pl.ds(low, high - low)], arecv_sem.at[at, piece])
                 apply(other_amps[at], plane_at(k) * nx + (x + 1 - core) % nx, far, False)
             elif kind == "return":
                 leave[...] = total[...].astype(jnp.bfloat16)
@@ -403,7 +416,7 @@
         scratch_shapes=[
             pltpu.VMEM((nocc, rows, naux * width), kind),
             pltpu.VMEM((nocc, 8, LANES), jnp.float32),
-            pltpu.VMEM((rows, rows), jnp.float32),
+            pltpu.VMEM((2, rows, rows), jnp.float32),
             pltpu.VMEM((tasks, rows, rows), jnp.bfloat16),
             pltpu.VMEM((tasks, rows, rows), jnp.bfloat16),
             pltpu.VMEM((rows, width), jnp.float32),
@@ -415,10 +428,11 @@
             dma((len(pieces), nocc * ny)),
             dma((16,)),
             dma((nocc,)),
-            dma((tasks,)),
-            dma((tasks,)),
+            dma((tasks, 4)),
+            dma((tasks, 4)),
             dma((len(pieces),)),
             dma((len(pieces),)),
+            dma,
             dma,
         ],
         compiler_params=pltpu.CompilerParams(

time: 54.5 us -> 49.4 us (0.906)
  Pallas kernels: 51 us -> 45.9 us
    pallas_call x1, Pallas kernels: 51 us -> 45.9 us  [gathered(): pl.pallas_call(functools.partial(gather_kernel, nz, nx, ny), out_shape=ja...]
where the time goes in v3:
time: 49.4 us; the launch traced here: 49.3 us
  Pallas kernels  45.9 us (93%)
  local copies, waits for them, and re-layouts  2.63 us (5%)
  between operations  0.69 us (1%)
    pallas_call x1, Pallas kernels, gathered(): pl.pallas_call(functools.partial(gather_kernel, nz, nx, ny), out_shape=ja...  45.9 us
    unnamed x5, local copies, waits for them, and re-layouts  2.49 us

profile of v3, /device:TPU:0, one launch (start us, length us, event | category | flops | bytes accessed | tf_op | source)
XLA Modules:
  0.0 49.3 jit_solution(5453580720082194596)
XLA Ops:
  0.7 0.0 copy-start.1
  0.7 0.7 %copy-done.1 = f32[448]{0:T(512)S(1)} copy-done((f32[448]{0:T(512)S(1)}, f32[448]{0:T(512)}, u32[]{:S(2)}) %copy-start.1) | copy-done | bytes 1816
  1.3 0.1 copy.4.col_ref
  1.5 0.0 copy-start
  1.5 1.0 %copy-done = bf16[1,448,384]{2,1,0:T(8,128)(2,1)S(1)} copy-done((bf16[1,448,384]{2,1,0:T(8,128)(2,1)S(1)}, bf16[1,448,384]{2,1,0:T(8,128)(2,1)}, u32[]{:S(2)}) %copy-start) | copy-done | bytes 344088
  2.5 45.9 %shard_map.37 = f32[448,384]{1,0:T(8,128)S(1)} custom-call(bf16[448,384]{1,0:T(8,128)(2,1)S(1)} %bitcast.7, f32[8,128]{1,0:T(8,128)S(1)} %broadcast_in_dim.17.e_ref, f32[448,1]{1,0:T(8,128)S(1)} %copy.4.col_ref, f32[1,448]{1,0:T(1,128)S(1)} %bitcast.9), custom_call_target="tpu_custom_call" | custom-call | tf_op jit(solution)/shard_map/pallas_call | solution.py:411
  48.4 0.8 %copy.7 = f32[1,448,384]{2,1,0:T(8,128)} copy(f32[1,448,384]{2,1,0:T(8,128)S(1)} %bitcast.6) | data formatting | bytes 1376256
  (1 shorter events, 0.0 us)
Async XLA Ops:
  0.7 0.7 %copy-start.1 = (f32[448]{0:T(512)S(1)}, f32[448]{0:T(512)}, u32[]{:S(2)}) copy-start(f32[448]{0:T(512)} %param.5) | copy-start | bytes 5380
  1.5 1.0 %copy-start = (bf16[1,448,384]{2,1,0:T(8,128)(2,1)S(1)}, bf16[1,448,384]{2,1,0:T(8,128)(2,1)}, u32[]{:S(2)}) copy-start(bf16[1,448,384]{2,1,0:T(8,128)(2,1)} %param.3) | copy-start | bytes 1032196

commit v4 on v3

--- a/solution.py
+++ b/solution.py
@@ -17,13 +17,14 @@
 HOP = 2.4
 AHEAD = 2.0
 SLACK = 0.0
-RETURN = 5.0
+RETURN = 3.5
+ALONE = (2,)
 LAST = 0
-MIRROR = 1.0
-MATMUL = 0.45
-ELEMENT = 0.25
-APPLY = 0.35
-EXCHANGE = 1.5
+MIRROR = 2.0
+MATMUL = 0.36
+ELEMENT = 0.08
+APPLY = 0.24
+EXCHANGE = 1.4
 STEP = {"x": (1, 0, 0), "y": (0, 1, 0), "+": (0, 0, 1), "-": (0, 0, -1)}
 BACK = {"x": "x", "y": "y", "+": "-", "-": "+"}
 ROUTES = (
@@ -130,13 +131,21 @@
     tasks, jobs = [], []
     work = [("open", 0, 0.0)] + [("matmul", part, MATMUL) for part in range(2)]
     work += [("element", part, ELEMENT) for part in range(4)] + [("mine", 0, APPLY)]
+
+    def add(when, rank, plane, far, dx, extra=()):
+        jobs.append((when, rank, len(tasks), work + list(extra)))
+        tasks.append((plane, far, dx))
+
     for plane in sorted({key[0] for key in ready}):
-        both = max(ready[plane, 0], ready[plane, 1])
         if inner and plane == 3:
-            jobs.append((max(both, ready[0, 0]), 0, len(tasks), list(work)))
-            tasks.append((plane, True))
-        jobs.append((max(both, ready[own, 0]), 2, len(tasks), list(work)))
-        tasks.append((plane, False))
+            order = sorted((max(ready[plane, dx], ready[0, 0]), dx) for dx in range(2))
+            add(*order[0][:1], 0, plane, True, order[0][1])
+            add(*order[1][:1], 0, plane, True, order[1][1], [("return", 0, 0.1)])
+        if plane in ALONE:
+            for dx in range(2):
+                add(max(ready[plane, dx], ready[own, 0]), 2, plane, False, dx)
+        else:
+            add(max(ready[plane, 0], ready[plane, 1], ready[own, 0]), 2, plane, False, None)
     steps, clock = [], 0.0
     while jobs:
         clock = max(clock, min(job[0] for job in jobs))
@@ -146,9 +155,8 @@
         clock += cost
         if not job[3]:
             jobs.remove(job)
-        if kind == "mine":
-            rest = [("other", 0, APPLY)] + ([("return", 0, 0.1)] if tasks[job[2]][1] else [])
-            jobs.append((clock + EXCHANGE, min(job[1], 1), job[2], rest))
+        if kind == "mine" and tasks[job[2]][2] is None:
+            jobs.append((clock + EXCHANGE, 1, job[2], [("other", 0, APPLY)]))
     return tasks, steps, clock
 
 
@@ -187,9 +195,9 @@
     return [event[2] for event in events], tasks
 
 
-def gather_kernel(nz, nx, ny, b_ref, e_ref, col_ref, row_ref, out_ref, blocks, energies, value, mine_amps, other_amps,
+def gather_kernel(nz, nx, ny, hbm_ref, occ_ref, row_ref, out_ref, b_ref, e_ref, col_ref, blocks, energies, value, mine_amps, other_amps,
                   total, leave, come, send_sem, recv_sem, msend_sem, mrecv_sem, esend_sem, erecv_sem,
-                  asend_sem, arecv_sem, fsend_sem, frecv_sem, keep_sem, unused_sem):
+                  asend_sem, arecv_sem, fsend_sem, frecv_sem, keep_sem, load_sem, unused_sem):
     rows, width = b_ref.shape
     occ, aux = lax.axis_index("occ"), lax.axis_index("aux")
     z, x = occ // nx, occ % nx
@@ -215,7 +223,8 @@
         return pl.ds(pl.multiple_of(shard_aux * width, width), width)
 
     keep = pltpu.make_async_copy(b_ref, blocks.at[occ, :, columns(aux)], keep_sem)
-    keep.start()
+    load = pltpu.make_async_copy(hbm_ref, b_ref, load_sem)
+    load.start()
     partner = (occ, y * CORES + (core + 1) % CORES)
     barrier = pltpu.get_barrier_semaphore()
     step_up = 1 - 2 * upper
@@ -232,6 +241,10 @@
     def _():
         pl.semaphore_signal(barrier, inc=1, device_id=((z - step_up) * nx + x, aux), device_id_type=MESH)
 
+    e_ref[...] = jnp.full(e_ref.shape, occ_ref[0], jnp.float32)
+    col_ref[...] = jnp.broadcast_to(row_ref[...], (8, rows)).T[:, 0:1]
+    load.wait()
+    keep.start()
     pl.semaphore_wait(barrier, len(near) + plane)
 
     def run(me):
@@ -330,13 +343,13 @@
             goal[...] = term if fresh else goal[...] + term
 
         def step(kind, at, part):
-            k, far = tasks[at]
+            k, far, dx = tasks[at]
             left = block_at(0, 0) if far else occ
-            right = plane_at(k) * nx + (x + core) % nx
+            right = plane_at(k) * nx + (x + (core if dx is None else dx)) % nx
             if kind == "open":
                 open_block(0, 0 if far else me)
-                open_block(0, k)
-                open_block(1, k)
+                for which in range(2) if dx is None else [dx]:
+                    open_block(which, k)
             elif kind == "matmul":
                 cut = rows // 2 // LANES * LANES + LANES if rows > LANES else rows
                 low, high = ((0, min(cut, rows)), (min(cut, rows), rows))[part]
@@ -352,12 +365,13 @@
                     numer = 2.0 * value[int(far), low:high, :] - value[int(far), :, low:high].T
                     denom = col_ref[low:high, :] + row_ref[...] - energies[left, 0:1, 0:1] - energies[right, 0:1, 0:1]
                     mine_amps[at, low:high, :] = (numer / denom).astype(jnp.bfloat16)
-                if part:
+                if part and dx is None:
                     hand_over(at, part - 1)
             elif kind == "mine":
                 apply(mine_amps[at], right, far, far not in started)
                 started[far] = True
-                hand_over(at, 3)
+                if dx is None:
+                    hand_over(at, 3)
             elif kind == "other":
                 size = -(-rows // (4 * LANES)) * LANES
                 for piece in range(4):
@@ -403,17 +417,19 @@
     nocc, naux = nz * nx, ny * CORES
     pieces = piece_rows(rows)
     copies = max(sum(event[0] == "send" for event in program_of(plane, pieces, width)[0]) for plane in range(2))
-    tasks = 5
-    energy = jnp.broadcast_to(occ_energy.reshape(1, 1), (8, LANES))
+    tasks = max(len(program_of(plane, pieces, width)[1]) for plane in range(2))
     vmem = pl.BlockSpec(memory_space=pltpu.VMEM)
     dma = pltpu.SemaphoreType.DMA
     kind = three_index.dtype
     out = pl.pallas_call(
         functools.partial(gather_kernel, nz, nx, ny),
         out_shape=jax.ShapeDtypeStruct((rows, width), jnp.float32),
-        in_specs=[vmem] * 4,
+        in_specs=[pl.BlockSpec(memory_space=pltpu.HBM), pl.BlockSpec(memory_space=pltpu.SMEM), vmem],
         out_specs=vmem,
         scratch_shapes=[
+            pltpu.VMEM((rows, width), kind),
+            pltpu.VMEM((8, LANES), jnp.float32),
+            pltpu.VMEM((rows, 1), jnp.float32),
             pltpu.VMEM((nocc, rows, naux * width), kind),
             pltpu.VMEM((nocc, 8, LANES), jnp.float32),
             pltpu.VMEM((2, rows, rows), jnp.float32),
@@ -434,11 +450,12 @@
             dma((len(pieces),)),
             dma,
             dma,
+            dma,
         ],
         compiler_params=pltpu.CompilerParams(
             collective_id=0, has_side_effects=True, vmem_limit_bytes=48 * 1024 * 1024
         ),
-    )(three_index[0], energy, vir_energy[:, None], vir_energy[None, :])
+    )(three_index[0], occ_energy, vir_energy[None, :])
     return out[None]
 
 

time: 49.4 us -> 47.2 us (0.955)
  Pallas kernels: 45.9 us -> 43.9 us
    pallas_call x1, Pallas kernels: 45.9 us -> 43.9 us  [gathered(): pl.pallas_call(functools.partial(gather_kernel, nz, nx, ny), out_shape=ja...]
where the time goes in v4:
time: 47.2 us; the launch traced here: 47.1 us
  Pallas kernels  43.9 us (93%)
  local copies, waits for them, and re-layouts  2.5 us (5%)
  between operations  0.67 us (1%)
    pallas_call x1, Pallas kernels, gathered(): pl.pallas_call(functools.partial(gather_kernel, nz, nx, ny), out_shape=ja...  43.9 us
    unnamed x5, local copies, waits for them, and re-layouts  2.5 us

profile of v4, /device:TPU:0, one launch (start us, length us, event | category | flops | bytes accessed | tf_op | source)
XLA Modules:
  0.0 47.1 jit_solution(15582081243062220385)
XLA Ops:
  0.7 0.0 copy-start.1
  0.7 0.7 %copy-done.1 = f32[448]{0:T(512)S(1)} copy-done((f32[448]{0:T(512)S(1)}, f32[448]{0:T(512)}, u32[]{:S(2)}) %copy-start.1) | copy-done | bytes 1816
  1.3 0.0 copy-start
  1.3 1.0 %copy-done = bf16[1,448,384]{2,1,0:T(8,128)(2,1)S(1)} copy-done((bf16[1,448,384]{2,1,0:T(8,128)(2,1)S(1)}, bf16[1,448,384]{2,1,0:T(8,128)(2,1)}, u32[]{:S(2)}) %copy-start) | copy-done | bytes 344088
  2.3 43.9 %shard_map.37 = f32[448,384]{1,0:T(8,128)S(1)} custom-call(bf16[448,384]{1,0:T(8,128)(2,1)S(1)} %bitcast.4, f32[1]{0:T(128)S(6)} %copy.5.occ_ref, f32[1,448]{1,0:T(1,128)S(1)} %bitcast.5), custom_call_target="tpu_custom_call" | custom-call | tf_op jit(solution)/shard_map/pallas_call | solution.py:424
  46.2 0.8 %copy.6 = f32[1,448,384]{2,1,0:T(8,128)} copy(f32[1,448,384]{2,1,0:T(8,128)S(1)} %bitcast.3) | data formatting | bytes 1376256
Async XLA Ops:
  0.7 0.7 %copy-start.1 = (f32[448]{0:T(512)S(1)}, f32[448]{0:T(512)}, u32[]{:S(2)}) copy-start(f32[448]{0:T(512)} %param.5) | copy-start | bytes 5380
  1.3 1.0 %copy-start = (bf16[1,448,384]{2,1,0:T(8,128)(2,1)S(1)}, bf16[1,448,384]{2,1,0:T(8,128)(2,1)}, u32[]{:S(2)}) copy-start(bf16[1,448,384]{2,1,0:T(8,128)(2,1)} %param.3) | copy-start | bytes 1032196

commit v5 on v4

--- a/solution.py
+++ b/solution.py
@@ -14,7 +14,7 @@
 GATHER_LIMIT = 24 * 1024 * 1024
 LANES = 128
 RATE = 46250.0
-HOP = 2.4
+HOP = 2.6
 AHEAD = 2.0
 SLACK = 0.0
 RETURN = 3.5
@@ -183,7 +183,7 @@
                 events.append((max(last, back + 0.01), 4, ("return", items[at][1])))
     for at, (source, piece, _) in enumerate(items[:plain]):
         if (at, chip) in arrivals:
-            when = min(arrivals[at, chip] + SLACK, first.get(at, 1e9))
+            when = 1.0 if source == chip else min(arrivals[at, chip] + SLACK, first.get(at, 1e9))
             events.append((when, 1, ("take", source, piece)))
     events += [(when, 3, ("step", *step)) for when, *step in steps]
     for away in range(4 if plane == 1 else 3):

time: 47.2 us -> 47.2 us (level)
  no operation moved by 1% of the time
where the time goes in v5:
time: 47.2 us; the launch traced here: 47.1 us
  Pallas kernels  43.9 us (93%)
  local copies, waits for them, and re-layouts  2.5 us (5%)
  between operations  0.67 us (1%)
    pallas_call x1, Pallas kernels, gathered(): pl.pallas_call(functools.partial(gather_kernel, nz, nx, ny), out_shape=ja...  43.9 us
    unnamed x5, local copies, waits for them, and re-layouts  2.5 us

profile of v5, /device:TPU:0, one launch (start us, length us, event | category | flops | bytes accessed | tf_op | source)
XLA Modules:
  0.0 47.1 jit_solution(5160392430842955441)
XLA Ops:
  0.7 0.0 copy-start.1
  0.7 0.7 %copy-done.1 = f32[448]{0:T(512)S(1)} copy-done((f32[448]{0:T(512)S(1)}, f32[448]{0:T(512)}, u32[]{:S(2)}) %copy-start.1) | copy-done | bytes 1816
  1.3 0.0 copy-start
  1.3 1.0 %copy-done = bf16[1,448,384]{2,1,0:T(8,128)(2,1)S(1)} copy-done((bf16[1,448,384]{2,1,0:T(8,128)(2,1)S(1)}, bf16[1,448,384]{2,1,0:T(8,128)(2,1)}, u32[]{:S(2)}) %copy-start) | copy-done | bytes 344088
  2.3 43.9 %shard_map.37 = f32[448,384]{1,0:T(8,128)S(1)} custom-call(bf16[448,384]{1,0:T(8,128)(2,1)S(1)} %bitcast.4, f32[1]{0:T(128)S(6)} %copy.5.occ_ref, f32[1,448]{1,0:T(1,128)S(1)} %bitcast.5), custom_call_target="tpu_custom_call" | custom-call | tf_op jit(solution)/shard_map/pallas_call | solution.py:424
  46.2 0.8 %copy.6 = f32[1,448,384]{2,1,0:T(8,128)} copy(f32[1,448,384]{2,1,0:T(8,128)S(1)} %bitcast.3) | data formatting | bytes 1376256
Async XLA Ops:
  0.7 0.7 %copy-start.1 = (f32[448]{0:T(512)S(1)}, f32[448]{0:T(512)}, u32[]{:S(2)}) copy-start(f32[448]{0:T(512)} %param.5) | copy-start | bytes 5380
  1.3 1.0 %copy-start = (bf16[1,448,384]{2,1,0:T(8,128)(2,1)S(1)}, bf16[1,448,384]{2,1,0:T(8,128)(2,1)}, u32[]{:S(2)}) copy-start(bf16[1,448,384]{2,1,0:T(8,128)(2,1)} %param.3) | copy-start | bytes 1032196

commit v6 on v5

--- a/solution.py
+++ b/solution.py
@@ -17,10 +17,10 @@
 HOP = 2.6
 AHEAD = 2.0
 SLACK = 0.0
-RETURN = 3.5
+RETURN = 3.8
 ALONE = (2,)
 LAST = 0
-MIRROR = 2.0
+MIRROR = 2.3
 MATMUL = 0.36
 ELEMENT = 0.08
 APPLY = 0.24

time: 47.2 us -> 47.3 us (level)
  no operation moved by 1% of the time
where the time goes in v6:
time: 47.3 us; the launch traced here: 47.1 us
  Pallas kernels  43.9 us (93%)
  local copies, waits for them, and re-layouts  2.5 us (5%)
  between operations  0.67 us (1%)
    pallas_call x1, Pallas kernels, gathered(): pl.pallas_call(functools.partial(gather_kernel, nz, nx, ny), out_shape=ja...  43.9 us
    unnamed x5, local copies, waits for them, and re-layouts  2.5 us

profile of v6, /device:TPU:0, one launch (start us, length us, event | category | flops | bytes accessed | tf_op | source)
XLA Modules:
  0.0 47.1 jit_solution(2611381347010305145)
XLA Ops:
  0.7 0.0 copy-start.1
  0.7 0.7 %copy-done.1 = f32[448]{0:T(512)S(1)} copy-done((f32[448]{0:T(512)S(1)}, f32[448]{0:T(512)}, u32[]{:S(2)}) %copy-start.1) | copy-done | bytes 1816
  1.3 0.0 copy-start
  1.3 1.0 %copy-done = bf16[1,448,384]{2,1,0:T(8,128)(2,1)S(1)} copy-done((bf16[1,448,384]{2,1,0:T(8,128)(2,1)S(1)}, bf16[1,448,384]{2,1,0:T(8,128)(2,1)}, u32[]{:S(2)}) %copy-start) | copy-done | bytes 344088
  2.3 43.9 %shard_map.37 = f32[448,384]{1,0:T(8,128)S(1)} custom-call(bf16[448,384]{1,0:T(8,128)(2,1)S(1)} %bitcast.4, f32[1]{0:T(128)S(6)} %copy.5.occ_ref, f32[1,448]{1,0:T(1,128)S(1)} %bitcast.5), custom_call_target="tpu_custom_call" | custom-call | tf_op jit(solution)/shard_map/pallas_call | solution.py:424
  46.2 0.8 %copy.6 = f32[1,448,384]{2,1,0:T(8,128)} copy(f32[1,448,384]{2,1,0:T(8,128)S(1)} %bitcast.3) | data formatting | bytes 1376256
Async XLA Ops:
  0.7 0.7 %copy-start.1 = (f32[448]{0:T(512)S(1)}, f32[448]{0:T(512)}, u32[]{:S(2)}) copy-start(f32[448]{0:T(512)} %param.5) | copy-start | bytes 5380
  1.3 1.0 %copy-start = (bf16[1,448,384]{2,1,0:T(8,128)(2,1)S(1)}, bf16[1,448,384]{2,1,0:T(8,128)(2,1)}, u32[]{:S(2)}) copy-start(bf16[1,448,384]{2,1,0:T(8,128)(2,1)} %param.3) | copy-start | bytes 1032196
